TPU v7x, 128 devices: a whole 4x4x4 slice. The times are simulated.
128 devices in a mesh: macro: 16 (over z, y), pool: 8 (over x, core).
Axes of the slice: x: 4, y: 4, z: 4, core: 2. Of those that a mesh axis runs over, the one named last changes fastest.
Arguments:
- history: float32 [729, 65536], P(None, ('macro', 'pool')), may hold values from -6 to 6
- yield_flags: int32 [729, 65536], P(None, ('macro', 'pool')), may hold values 0 or 1
- strain: float32 [6, 65536], P(None, ('macro', 'pool')), may hold values from -6 to 6
- qp_to_rve: int32 [128, 512], P(('macro', 'pool')), may hold values from 0 to 511, each once within a row
- new_owner: int32 [65536, 1], P(('macro', 'pool')), may hold values from 0 to 127; in each aligned block of 512 rows (0 to 511, 512 to 1023, ...) at most 8 rows name the same one
- stiffness: float32 [9, 9, 81, 81], replicated, as said below
- pattern: int32 [9, 9], replicated, may hold values from 0 to 1, as said below
- coupling: float32 [3, 6, 729], replicated, as said below
- plastic_dir: float32 [3, 729], replicated, may hold values from -6 to 6
Outputs:
- new_history: float32 [729, 131072], P(None, ('macro', 'pool'))
- stress: float32 [6, 65536], P(None, ('macro', 'pool'))
Inputs may be any that keep to these rules, and one draw needn't show every extreme that they name: `new_owner`: among the rows of one device no owner is named more than 8 times, a bound that some block reaches. `qp_to_rve`: each row is a permutation of 0 to 511. `pattern`: Symmetric, with ones on the diagonal. stiffness[a, b] is the transpose of stiffness[b, a]; diagonal entries of diagonal blocks lie in 0.5 to 1.5, all others in 0 to 0.032. `coupling`: entries lie in -5.7 to 6.3.
All inputs are finite; a program needn't handle non-finite values. No bound on the sum of `yield_flags` on one device may be relied on, other than what follows from the above.
Results may differ from a plain program's by a relative error of at most 0.0003.
Values sent between devices are 32-bit elements; how exact they have to be, the bound alone decides.
A program may use at most 128 MiB of HBM per device.

v0:
```python
import functools
import math

import jax
import jax.numpy as jnp
from jax import lax
from jax.experimental import pallas as pl
from jax.experimental.pallas import tpu as pltpu
from jax.sharding import PartitionSpec as P

ITERS = 3
NB = 9
BLK = 81
COMP = 3
VOIGT = 6
NODES = NB * BLK
NP = 768
RV = 512
BW = 128
NBLK = RV // BW
DEV = 128
CAP = 8
CH = 64
STRIDE = 53
LOG = pl.DeviceIdType.LOGICAL
F32 = jnp.float32
BF = jnp.bfloat16


def split2(x):
    hi = x.astype(BF)
    return hi, (x - hi.astype(F32)).astype(BF)


def split3(x):
    hi = x.astype(BF)
    rest = x - hi.astype(F32)
    mid = rest.astype(BF)
    return hi, mid, (rest - mid.astype(F32)).astype(BF)


def dot(a, b):
    return jnp.dot(a, b, preferred_element_type=F32)


def to_columns(row):
    return jnp.transpose(jnp.broadcast_to(row, (BW, RV)))


def iota(shape, dim):
    return lax.broadcasted_iota(jnp.int32, shape, dim).astype(F32)


def kernel(
    hist_hbm, flag_hbm, strain_hbm, qp_hbm, owner_hbm, stiff_hbm, pat_ref, coup_hbm, plast_hbm,
    out_ref, stress_ref,
    hist_v, flag_v, strain_v, qp_v, owner_v, stiff_v, coup_v, plast_v,
    k32, kk, hcat, fcat, pos, slot, qcol, slotrow, s24, ct, gmat, pb,
    w_s, h_s, x_s, r_s, d_s, im_s, dd, ycat, ucat, stress_acc, ship, recv,
    in_sem, loc_sem, send_sem, recv_sem,
):
    me = lax.axis_index("macro") * 8 + lax.axis_index("pool")
    pairs = (
        (owner_hbm, owner_v), (qp_hbm, qp_v), (stiff_hbm, stiff_v), (hist_hbm, hist_v),
        (flag_hbm, flag_v), (strain_hbm, strain_v), (coup_hbm, coup_v), (plast_hbm, plast_v),
    )
    loads = [pltpu.make_async_copy(a, b, in_sem.at[i]) for i, (a, b) in enumerate(pairs)]
    for load in loads:
        load.start()

    barrier = pltpu.get_barrier_semaphore()

    def greet(i, carry):
        pl.semaphore_signal(barrier, inc=1, device_id=lax.rem(me + i, DEV), device_id_type=LOG)
        return carry

    lax.fori_loop(1, DEV, greet, 0)

    loads[0].wait()
    loads[1].wait()
    owner_row = owner_v[...].astype(F32)
    owner_col = to_columns(owner_row)
    qcol[...] = to_columns(qp_v[...].astype(F32))
    e_col = iota((RV, BW), 0)
    rank_part = jnp.zeros((RV, BW), F32)
    rank_rows = []
    for t in range(NBLK):
        e_row = iota((RV, BW), 1) + float(t * BW)
        same = owner_col == owner_row[:, t * BW : (t + 1) * BW]
        rank_part += jnp.where(same & (e_row < e_col), 1.0, 0.0)
        rank_rows.append(
            jnp.sum(jnp.where(same & (e_col < e_row), 1.0, 0.0), axis=0, keepdims=True)
        )
    rank_col = jnp.broadcast_to(jnp.sum(rank_part, axis=1, keepdims=True), (RV, BW))
    key_col = rank_col * float(RV) - e_col
    pos_part = jnp.zeros((RV, BW), F32)
    for t in range(NBLK):
        key_row = rank_rows[t] * float(RV) - (iota((1, BW), 1) + float(t * BW))
        pos_part += jnp.where(key_row > key_col, 1.0, 0.0)
    pos[...] = jnp.broadcast_to(jnp.sum(pos_part, axis=1, keepdims=True), (RV, BW))
    slot[...] = owner_col * float(CAP) + rank_col
    slotrow[...] = jnp.full(slotrow.shape, -1.0, F32)

    k32[...] = jnp.zeros_like(k32)
    loads[2].wait()
    for a in range(NB):
        row = [stiff_v[a, b] * pat_ref[a, b].astype(F32) for b in range(NB)]
        k32[pl.ds(a * BLK, BLK), pl.ds(0, NODES)] = jnp.concatenate(row, axis=1)

    def split_k(i, carry):
        rows = pl.ds(pl.multiple_of(i * CH, CH), CH)
        hi, lo = split2(k32[rows, :])
        kk[rows, pl.ds(0, NP)] = hi
        kk[rows, pl.ds(NP, NP)] = hi
        kk[rows, pl.ds(2 * NP, NP)] = lo
        return carry

    lax.fori_loop(0, NP // CH, split_k, 0)

    loads[3].wait()
    loads[4].wait()
    hcat[pl.ds(NP - 64, 64), :] = jnp.zeros((64, 2 * RV), BF)
    fcat[pl.ds(NP - 64, 64), :] = jnp.zeros((64, RV), BF)

    def split_h(i, carry):
        rows = pl.ds(pl.multiple_of(i * CH, CH), CH)
        hi, lo = split2(hist_v[rows, :])
        hcat[rows, pl.ds(0, RV)] = hi
        hcat[rows, pl.ds(RV, RV)] = lo
        fcat[rows, :] = flag_v[rows, :].astype(F32).astype(BF)
        return carry

    whole = NODES // CH
    lax.fori_loop(0, whole, split_h, 0)
    rest = pl.ds(whole * CH, NODES - whole * CH)
    hi, lo = split2(hist_v[rest, :])
    hcat[rest, pl.ds(0, RV)] = hi
    hcat[rest, pl.ds(RV, RV)] = lo
    fcat[rest, :] = flag_v[rest, :].astype(F32).astype(BF)

    for i in range(5, 8):
        loads[i].wait()
    two = jnp.zeros((2, RV), F32)
    s24[...] = jnp.concatenate(
        [p.astype(F32) for p in split3(jnp.concatenate([strain_v[...], two], axis=0))], axis=0
    ).astype(BF)
    edge = jnp.zeros((2, NODES), F32)
    coup = [jnp.concatenate([coup_v[c], edge], axis=0) for c in range(COMP)]
    pad = jnp.zeros((CAP, NP - NODES), F32)
    coup = [jnp.concatenate([c, pad], axis=1) for c in coup]
    chi = [c.astype(BF).astype(F32) for c in coup]
    clo = [c - h for c, h in zip(coup, chi)]
    ct[...] = jnp.transpose(
        jnp.concatenate(chi + clo + chi + [jnp.zeros((BW - 72, NP), F32)], axis=0)
    ).astype(BF)
    for c in range(COMP):
        gmat[:, pl.ds(c * NP, NP)] = jnp.concatenate([chi[c], clo[c]], axis=0).astype(BF)
        line = jnp.concatenate([plast_v[pl.ds(c, 1), :], pad[0:1]], axis=1)
        pb[c] = jnp.transpose(jnp.broadcast_to(line, (BW, NP)))
    stress_acc[...] = jnp.zeros_like(stress_acc)
    ucat[...] = jnp.zeros_like(ucat)

    def chunks(body, init):
        def step(i, carry):
            return body(pl.ds(pl.multiple_of(i * CH, CH), CH), i, carry)

        return lax.fori_loop(0, NP // CH, step, init)

    def fold(v):
        return jnp.sum(v.reshape(CH // 8, 8, BW), axis=0)

    zero8 = jnp.zeros((8, BW), F32)

    def block(b, carry):
        lane = iota((1, BW), 1) + (b * BW).astype(F32)
        chosen = pos[...] == lane
        e_row = jnp.sum(jnp.where(chosen, iota((RV, BW), 0), 0.0), axis=0, keepdims=True)
        s_row = jnp.sum(jnp.where(chosen, slot[...], 0.0), axis=0, keepdims=True)
        slotrow[:, pl.ds(pl.multiple_of(b * BW, BW), BW)] = jnp.broadcast_to(s_row, (8, BW))
        perm = jnp.where(chosen, 1.0, 0.0).astype(BF)
        serves = jnp.where(qcol[...] == e_row, 1.0, 0.0).astype(BF)
        h_s[...] = dot(hcat[...], jnp.concatenate([perm, perm], axis=0))
        w_s[...] = dot(fcat[...], perm)
        parts = dot(s24[...], serves)
        strain = parts[0:8] + parts[8:16] + parts[16:24]
        sh = strain.astype(BF).astype(F32)
        sl = strain - sh
        cols = []
        for c in range(COMP):
            rows = [zero8] * (BW // 8)
            rows[c], rows[3 + c], rows[6 + c] = sh, sh, sl
            cols.append(jnp.concatenate(rows, axis=0))
        drive = jnp.concatenate(cols, axis=1).astype(BF)
        im_s[...] = dot(ct[...], drive)

        def source(rows, i, rr):
            h = h_s[rows, :]
            h2 = h * h
            w = w_s[rows, :] * h2 / (1.0 + h2)
            w_s[rows, :] = w
            wh = w * h
            for c in range(COMP):
                lanes = pl.ds(c * BW, BW)
                v = im_s[rows, lanes] - wh * pb[c, rows, :]
                x_s[rows, lanes] = jnp.zeros((CH, BW), F32)
                r_s[rows, lanes] = v
                d_s[rows, lanes] = v
                hi, lo = split2(v)
                dd[pl.ds(pl.multiple_of(i * CH, CH), CH), lanes] = hi
                dd[pl.ds(pl.multiple_of(NP + i * CH, CH), CH), lanes] = lo
                dd[pl.ds(pl.multiple_of(2 * NP + i * CH, CH), CH), lanes] = hi
                rr = rr + fold(v * v)
            return rr

        rr0 = jnp.sum(chunks(source, zero8), axis=0, keepdims=True)

        def iterate(it, rr):
            im_s[...] = dot(kk[...], dd[...])

            def apply(rows, i, acc):
                tan = 1.5 - w_s[rows, :]
                for c in range(COMP):
                    lanes = pl.ds(c * BW, BW)
                    d = d_s[rows, lanes]
                    im = im_s[rows, lanes] + tan * d
                    im_s[rows, lanes] = im
                    acc = acc + fold(d * im)
                return acc

            energy = jnp.sum(chunks(apply, zero8), axis=0, keepdims=True)
            size = rr / jnp.maximum(energy, 1.0)

            def advance(rows, i, acc):
                for c in range(COMP):
                    lanes = pl.ds(c * BW, BW)
                    x_s[rows, lanes] = x_s[rows, lanes] + size * d_s[rows, lanes]
                    r = r_s[rows, lanes] - size * im_s[rows, lanes]
                    r_s[rows, lanes] = r
                    acc = acc + fold(r * r)
                return acc

            after = jnp.sum(chunks(advance, zero8), axis=0, keepdims=True)
            ratio = after / jnp.maximum(rr, 1.0)

            def turn(rows, i, acc):
                for c in range(COMP):
                    lanes = pl.ds(c * BW, BW)
                    d = r_s[rows, lanes] + ratio * d_s[rows, lanes]
                    d_s[rows, lanes] = d
                    hi, lo = split2(d)
                    dd[pl.ds(pl.multiple_of(i * CH, CH), CH), lanes] = hi
                    dd[pl.ds(pl.multiple_of(NP + i * CH, CH), CH), lanes] = lo
                    dd[pl.ds(pl.multiple_of(2 * NP + i * CH, CH), CH), lanes] = hi
                return acc

            @pl.when(it < ITERS - 1)
            def _():
                chunks(turn, 0)

            return after

        lax.fori_loop(0, ITERS, iterate, rr0)

        def finish(rows, i, acc):
            w = w_s[rows, :]
            tan = 1.5 - w
            flow = jnp.zeros((CH, BW), F32)
            for c in range(COMP):
                x = x_s[rows, pl.ds(c * BW, BW)]
                flow = flow + pb[c, rows, :] * x
                hi, lo = split2(tan * x)
                there = pl.ds(pl.multiple_of(c * NP + i * CH, CH), CH)
                ycat[there, pl.ds(0, BW)] = hi
                ycat[there, pl.ds(BW, BW)] = lo
            h_s[rows, :] = h_s[rows, :] + w * flow
            return acc

        chunks(finish, 0)

        hi, lo = split2(jnp.transpose(h_s[...]))
        ucat[pl.ds(pl.multiple_of(b * BW, BW), BW), :] = hi
        ucat[pl.ds(pl.multiple_of(RV + b * BW, BW), BW), :] = lo
        first = 2.0 * (NBLK - 1 - b).astype(F32)
        t8 = float(CAP) * iota((DEV, RV), 0) + first
        srow = slotrow[0:1, :]
        place = jnp.concatenate(
            [jnp.where(srow == t8, 1.0, 0.0), jnp.where(srow == t8 + 1.0, 1.0, 0.0)], axis=0
        ).astype(BF)
        moved = dot(jnp.concatenate([place, place], axis=1), ucat[...])

        for k in range(NBLK):
            j = NBLK - 1 - k

            @pl.when(b == k)
            def _():
                ship[:, 2 * j, :] = moved[0:DEV]
                ship[:, 2 * j + 1, :] = moved[DEV:]
                if k == 0:
                    pl.semaphore_wait(barrier, DEV - 1)

                def send(i, c):
                    peer = lax.rem(me + i * STRIDE, DEV)
                    pltpu.make_async_remote_copy(
                        src_ref=ship.at[peer, pl.ds(2 * j, 2)],
                        dst_ref=recv.at[me, pl.ds(2 * j, 2)],
                        send_sem=send_sem.at[k],
                        recv_sem=recv_sem.at[k],
                        device_id=peer,
                        device_id_type=LOG,
                    ).start()
                    return c

                lax.fori_loop(1, DEV, send, 0)

        both = dot(gmat[...], ycat[...])
        delta = both[0:8, 0:BW] + both[8:16, 0:BW] + both[0:8, BW : 2 * BW]
        stress = strain + delta * (1.0 / math.sqrt(COMP * NODES))
        st24 = jnp.concatenate([p.astype(F32) for p in split3(stress)], axis=0).astype(BF)
        back = lax.dot_general(
            st24, serves, (((1,), (1,)), ((), ())), preferred_element_type=F32
        )
        stress_acc[...] += back[0:8] + back[8:16] + back[16:24]
        return carry

    lax.fori_loop(0, NBLK, block, 0)
    own = pltpu.make_async_copy(ship.at[me], recv.at[me], loc_sem)
    own.start()
    stress_ref[...] = stress_acc[0:VOIGT, :]
    own.wait()
    for k in range(NBLK):
        two_rows = pl.ds(2 * (NBLK - 1 - k), 2)
        some = pl.ds(0, DEV - 1)
        pltpu.make_async_copy(ship.at[some, two_rows], recv.at[some, two_rows], recv_sem.at[k]).wait()
        pltpu.make_async_copy(ship.at[some, two_rows], recv.at[some, two_rows], send_sem.at[k]).wait()

    def turn_out(i, carry):
        piece = recv[pl.ds(pl.multiple_of(i * 16, 16), 16)].reshape(BW, NP)
        out_ref[:, pl.ds(pl.multiple_of(i * BW, BW), BW)] = jnp.transpose(piece)[0:NODES]
        return carry

    lax.fori_loop(0, DEV // 16, turn_out, 0)


def shards(
    history, yield_flags, strain, qp_to_rve, new_owner, stiffness, pattern, coupling, plastic_dir
):
    owner = new_owner.reshape(1, RV)
    hbm = pl.BlockSpec(memory_space=pl.ANY)
    vmem = pl.BlockSpec(memory_space=pltpu.VMEM)
    v = pltpu.VMEM
    return pl.pallas_call(
        kernel,
        out_shape=(
            jax.ShapeDtypeStruct((NODES, DEV * CAP), F32),
            jax.ShapeDtypeStruct((VOIGT, RV), F32),
        ),
        in_specs=[hbm] * 6 + [pl.BlockSpec(memory_space=pltpu.SMEM)] + [hbm] * 2,
        out_specs=(vmem, vmem),
        scratch_shapes=[
            v((NODES, RV), F32), v((NODES, RV), jnp.int32), v((VOIGT, RV), F32),
            v((1, RV), jnp.int32), v((1, RV), jnp.int32), v((NB, NB, BLK, BLK), F32),
            v((COMP, VOIGT, NODES), F32), v((COMP, NODES), F32),
            v((NP, NP), F32), v((NP, 3 * NP), BF), v((NP, 2 * RV), BF), v((NP, RV), BF),
            v((RV, BW), F32), v((RV, BW), F32), v((RV, BW), F32), v((8, RV), F32),
            v((24, RV), BF), v((NP, BW), BF), v((16, COMP * NP), BF), v((COMP, NP, BW), F32),
            v((NP, BW), F32), v((NP, BW), F32), v((NP, COMP * BW), F32), v((NP, COMP * BW), F32),
            v((NP, COMP * BW), F32), v((NP, COMP * BW), F32), v((3 * NP, COMP * BW), BF),
            v((COMP * NP, 2 * BW), BF), v((2 * RV, NP), BF), v((8, RV), F32),
            v((DEV, CAP, NP), F32), v((DEV, CAP, NP), F32),
            pltpu.SemaphoreType.DMA((8,)), pltpu.SemaphoreType.DMA(()),
            pltpu.SemaphoreType.DMA((NBLK,)), pltpu.SemaphoreType.DMA((NBLK,)),
        ],
        compiler_params=pltpu.CompilerParams(
            collective_id=0, has_side_effects=True, vmem_limit_bytes=56 * 1024 * 1024
        ),
        name="micro_newton",
    )(
        history, yield_flags, strain, qp_to_rve, owner, stiffness, pattern, coupling, plastic_dir
    )


def solution(mesh):
    both = ("macro", "pool")
    return jax.shard_map(
        shards,
        mesh=mesh,
        in_specs=(
            P(None, both), P(None, both), P(None, both), P(both, None), P(both, None),
            P(), P(), P(), P(),
        ),
        out_specs=(P(None, both), P(None, both)),
        check_vma=False,
    )
```

profile of v0, /device:TPU:1, one launch (start us, length us, event | category | flops | bytes accessed | tf_op | source)
XLA Modules:
  0.0 88.5 jit_solution(6176864503202829134)
XLA Ops:
  0.6 83.4 %micro_newton.1 = (f32[729,1024]{1,0:T(8,128)}, f32[6,512]{1,0:T(8,128)}) custom-call(f32[729,512]{1,0:T(8,128)} %hist_hbm.1, s32[729,512]{1,0:T(8,128)} %flag_hbm.1, f32[6,512]{1,0:T(8,128)} %strain_hbm.1, s32[1,512]{1,0:T(1,128)} %qp_hbm.1, s32[1,512]{1,0:T(1,128)} %bitcast.1, f32[9,9,81,81]{3,2,1,0:T(8,128)} %stiff_hbm.1, s32[9,9]{1,0:T(8,128)} %pat_ref.1, ...), custom_call_target="tpu_custom_call" | custom-call | tf_op jit(solution)/shard_map/micro_newton/pallas_call | solution.py:351
  84.0 0.0 copy-start
  84.0 3.9 %copy.13 = f32[729,1024]{1,0:T(8,128)} copy(f32[729,1024]{1,0:T(8,128)} %get-tuple-element.4) | data formatting | bytes 5971968
  87.9 0.0 copy-done
  87.9 0.6 copy.14
Async XLA Ops:
  84.0 3.9 %copy-start = (f32[6,512]{1,0:T(8,128)S(1)}, f32[6,512]{1,0:T(8,128)}, u32[]{:S(2)}) copy-start(f32[6,512]{1,0:T(8,128)} %get-tuple-element.5) | copy-start | bytes 36868
where the time goes:
time: 88.7 us; the launch traced here: 88.5 us
  Pallas kernels  83.4 us (94%)
  local copies, waits for them, and re-layouts  4.48 us (5%)
    pallas_call x1, Pallas kernels, shards(): pl.pallas_call(kernel, out_shape=(jax.ShapeDtypeStruct((NODES, DEV * CAP)...  83.4 us
    unnamed x4, local copies, waits for them, and re-layouts  4.48 us

commit v1 on v0

v1 whole, which is shorter than its diff:
```python
import functools
import math

import jax
import jax.numpy as jnp
from jax import lax
from jax.experimental import pallas as pl
from jax.experimental.pallas import tpu as pltpu
from jax.sharding import PartitionSpec as P

ITERS = 3
NB = 9
BLK = 81
COMP = 3
VOIGT = 6
NODES = NB * BLK
NP = 768
RV = 512
BW = 128
NBLK = RV // BW
DEV = 128
CAP = 8
CH = 64
RC = 8
UNROLL = 16
STRIDE = 53
LOG = pl.DeviceIdType.LOGICAL
F32 = jnp.float32
BF = jnp.bfloat16


def split2(x):
    hi = x.astype(BF)
    return hi, (x - hi.astype(F32)).astype(BF)


def split3(x):
    hi = x.astype(BF)
    rest = x - hi.astype(F32)
    mid = rest.astype(BF)
    return hi, mid, (rest - mid.astype(F32)).astype(BF)


def dot(a, b):
    return jnp.dot(a, b, preferred_element_type=F32)


def to_columns(row):
    return jnp.transpose(jnp.broadcast_to(row, (BW, RV)))


def iota(shape, dim):
    return lax.broadcasted_iota(jnp.int32, shape, dim).astype(F32)


def dot_t(a, b):
    return lax.dot_general(a, b, (((1,), (1,)), ((), ())), preferred_element_type=F32)


def stack(parts):
    return jnp.concatenate([p.astype(F32) for p in parts], axis=0).astype(BF)


def kernel(
    hist_hbm, flag_hbm, strain_hbm, qp_hbm, owner_hbm, stiff_hbm, pat_ref, coup_hbm, plast_hbm,
    out_ref, stress_ref,
    hist_v, flag_v, strain_v, qp_v, owner_v, stiff_v, coup_v, plast_v,
    k32, kk, hcat, fcat, slotrow, s32, permt, servest, drive, prow, gmat,
    h_s, w_s, r0_s, r1_s, r2_s, im0_s, y_s, dd, ycat, ucat, coef, ship, recv,
    in_sem, loc_sem, send_sem, recv_sem,
):
    me = lax.axis_index("macro") * 8 + lax.axis_index("pool")
    pairs = (
        (owner_hbm, owner_v), (qp_hbm, qp_v), (stiff_hbm, stiff_v), (hist_hbm, hist_v),
        (flag_hbm, flag_v), (strain_hbm, strain_v), (coup_hbm, coup_v), (plast_hbm, plast_v),
    )
    loads = [pltpu.make_async_copy(a, b, in_sem.at[i]) for i, (a, b) in enumerate(pairs)]
    for load in loads:
        load.start()

    barrier = pltpu.get_barrier_semaphore()

    def greet(i, carry):
        pl.semaphore_signal(barrier, inc=1, device_id=lax.rem(me + i, DEV), device_id_type=LOG)
        return carry

    lax.fori_loop(1, DEV, greet, 0)

    loads[0].wait()
    loads[1].wait()
    owner_row = owner_v[...].astype(F32)
    owner_col = to_columns(owner_row)
    qp_row = qp_v[...].astype(F32)
    e_col = iota((RV, BW), 0)
    rank_part = jnp.zeros((RV, BW), F32)
    rank_rows = []
    for t in range(NBLK):
        e_row = iota((RV, BW), 1) + float(t * BW)
        same = owner_col == owner_row[:, t * BW : (t + 1) * BW]
        rank_part += jnp.where(same & (e_row < e_col), 1.0, 0.0)
        rank_rows.append(
            jnp.sum(jnp.where(same & (e_col < e_row), 1.0, 0.0), axis=0, keepdims=True)
        )
    rank_col = jnp.broadcast_to(jnp.sum(rank_part, axis=1, keepdims=True), (RV, BW))
    key_col = rank_col * float(RV) - e_col
    e_part = jnp.zeros((RV, BW), F32)
    slot_part = jnp.zeros((RV, BW), F32)
    for t in range(NBLK):
        lanes = pl.ds(t * BW, BW)
        e_row = iota((1, BW), 1) + float(t * BW)
        key_row = rank_rows[t] * float(RV) - e_row
        pos_row = jnp.sum(jnp.where(key_col > key_row, 1.0, 0.0), axis=0, keepdims=True)
        slot_row = owner_row[:, t * BW : (t + 1) * BW] * float(CAP) + rank_rows[t]
        chosen = iota((RV, BW), 0) == pos_row
        e_part += jnp.where(chosen, e_row, 0.0)
        slot_part += jnp.where(chosen, slot_row, 0.0)
        one = jnp.where(chosen, 1.0, 0.0).astype(BF)
        permt[:, lanes] = one
        permt[:, pl.ds(RV + t * BW, BW)] = one
    e_of = jnp.broadcast_to(jnp.sum(e_part, axis=1, keepdims=True), (RV, BW))
    slot_of = jnp.broadcast_to(jnp.sum(slot_part, axis=1, keepdims=True), (RV, BW))
    slotrow[...] = jnp.transpose(slot_of)[0:8]
    for t in range(NBLK):
        lanes = pl.ds(t * BW, BW)
        hit = e_of == qp_row[:, t * BW : (t + 1) * BW]
        servest[:, lanes] = jnp.where(hit, 1.0, 0.0).astype(BF)

    for i in range(5, 8):
        loads[i].wait()
    shi, smid, slo = split3(jnp.concatenate([strain_v[...], jnp.zeros((2, RV), F32)], axis=0))
    s32[...] = stack([shi, shi, smid, slo])
    strain_t = dot_t(servest[...], s32[...]).astype(BF)
    edge = jnp.zeros((2, NODES), F32)
    pad = jnp.zeros((CAP, NP - NODES), F32)
    cols = []
    for c in range(COMP):
        coup = jnp.concatenate([jnp.concatenate([coup_v[c], edge], axis=0), pad], axis=1)
        chi = coup.astype(BF).astype(F32)
        clo = coup - chi
        gmat[:, pl.ds(c * NP, NP)] = jnp.concatenate([chi, clo], axis=0).astype(BF)
        cols.append(jnp.concatenate([chi, clo, chi, jnp.zeros((8, NP), F32)], axis=0))
        line = jnp.concatenate([plast_v[pl.ds(c, 1), :], pad[0:1]], axis=1)
        prow[c] = jnp.broadcast_to(line, (8, NP))
    drive[...] = dot(strain_t, jnp.concatenate(cols, axis=1).astype(BF))

    loads[3].wait()
    loads[4].wait()
    hcat[pl.ds(NP - 64, 64), :] = jnp.zeros((64, 2 * RV), BF)
    fcat[pl.ds(NP - 64, 64), :] = jnp.zeros((64, RV), BF)

    def split_h(i, carry):
        rows = pl.ds(pl.multiple_of(i * CH, CH), CH)
        hi, lo = split2(hist_v[rows, :])
        hcat[rows, pl.ds(0, RV)] = hi
        hcat[rows, pl.ds(RV, RV)] = lo
        fcat[rows, :] = flag_v[rows, :].astype(F32).astype(BF)
        return carry

    whole = NODES // CH
    lax.fori_loop(0, whole, split_h, 0)
    rest = pl.ds(whole * CH, NODES - whole * CH)
    hi, lo = split2(hist_v[rest, :])
    hcat[rest, pl.ds(0, RV)] = hi
    hcat[rest, pl.ds(RV, RV)] = lo
    fcat[rest, :] = flag_v[rest, :].astype(F32).astype(BF)
    h_s[...] = dot_t(permt[...], hcat[...])
    w_s[...] = dot_t(permt[:, 0:RV], fcat[...])

    k32[...] = jnp.zeros_like(k32)
    loads[2].wait()
    for a in range(NB):
        row = [stiff_v[a, b] * pat_ref[a, b].astype(F32) for b in range(NB)]
        k32[pl.ds(a * BLK, BLK), pl.ds(0, NODES)] = jnp.concatenate(row, axis=1)

    def split_k(i, carry):
        hi, lo = split2(k32[pl.ds(pl.multiple_of(i * CH, CH), CH), :])
        kk[pl.ds(pl.multiple_of(i * CH, CH), CH), :] = hi
        kk[pl.ds(pl.multiple_of(NP + i * CH, CH), CH), :] = lo
        kk[pl.ds(pl.multiple_of(2 * NP + i * CH, CH), CH), :] = hi
        return carry

    lax.fori_loop(0, NP // CH, split_k, 0)
    ucat[...] = jnp.zeros_like(ucat)

    def chunks(body):
        def step(i, carry):
            body(i)
            return carry

        lax.fori_loop(0, BW // RC, step, 0, unroll=UNROLL)

    def at(base, i):
        return pl.ds(pl.multiple_of(base + i * RC, RC), RC)

    def total(acc):
        part = acc[:, 0:128]
        for k in range(1, NP // 128):
            part = part + acc[:, k * 128 : (k + 1) * 128]
        return jnp.sum(part, axis=1, keepdims=True)

    def keep(k, i, col):
        coef[k, at(0, i), :] = jnp.broadcast_to(col, (RC, 128))

    def kept(k, i):
        return coef[k, at(0, i), 0:1]

    def put(rows, v, low=True):
        hi = v.astype(BF).astype(F32)
        dd[rows, pl.ds(0, NP)] = hi
        if low:
            dd[rows, pl.ds(NP, NP)] = v - hi

    def block(b, carry):
        base = b * BW

        def source(i):
            here = at(base, i)
            h = h_s[here, :]
            h2 = h * h
            w = w_s[here, :] * h2 / (1.0 + h2)
            w_s[here, :] = w
            wh = w * h
            acc = jnp.zeros((RC, NP), F32)
            for c in range(COMP):
                rows = at(c * BW, i)
                v = drive[here, pl.ds(c * NP, NP)] - wh * prow[c, 0:RC, :]
                r0_s[rows, :] = v
                put(rows, v)
                acc = acc + v * v
            keep(0, i, total(acc))

        chunks(source)

        def product(parts):
            left = dd[...].astype(BF)
            hi = left[:, 0:NP]
            cat = [hi, hi] + ([left[:, NP:]] if parts == 3 else [])
            return dot(jnp.concatenate(cat, axis=1), kk[0 : parts * NP, :])

        im0_s[...] = product(3)

        def first(i):
            tan = 1.5 - w_s[at(base, i), :]
            acc = jnp.zeros((RC, NP), F32)
            ims = []
            for c in range(COMP):
                rows = at(c * BW, i)
                r = r0_s[rows, :]
                im = im0_s[rows, :] + tan * r
                im0_s[rows, :] = im
                ims.append(im)
                acc = acc + r * im
            rr = kept(0, i)
            size = rr / jnp.maximum(total(acc), 1.0)
            acc = jnp.zeros((RC, NP), F32)
            for c in range(COMP):
                rows = at(c * BW, i)
                r = r0_s[rows, :] - size * ims[c]
                r1_s[rows, :] = r
                put(rows, r)
                acc = acc + r * r
            after = total(acc)
            keep(1, i, size)
            keep(2, i, after)
            keep(3, i, after / jnp.maximum(rr, 1.0))

        chunks(first)
        y_s[...] = product(3)

        def second(i):
            tan = 1.5 - w_s[at(base, i), :]
            ratio = kept(3, i)
            acc = jnp.zeros((RC, NP), F32)
            ims = []
            for c in range(COMP):
                rows = at(c * BW, i)
                r = r1_s[rows, :]
                im = y_s[rows, :] + tan * r + ratio * im0_s[rows, :]
                ims.append(im)
                acc = acc + (r + ratio * r0_s[rows, :]) * im
            rr = kept(2, i)
            energy = total(acc)
            size = rr / jnp.maximum(energy, 1.0)
            sq = jnp.zeros((RC, NP), F32)
            cross = jnp.zeros((RC, NP), F32)
            for c in range(COMP):
                rows = at(c * BW, i)
                r = r1_s[rows, :] - size * ims[c]
                r2_s[rows, :] = r
                put(rows, r, low=False)
                sq = sq + r * r
                cross = cross + r * ims[c]
            after = total(sq)
            ratio = after / jnp.maximum(rr, 1.0)
            keep(4, i, size)
            keep(5, i, after)
            keep(6, i, ratio)
            keep(7, i, total(tan * sq) + ratio * (2.0 * total(cross) + ratio * energy))

        chunks(second)
        y_s[...] = product(2)

        def last(i):
            here = at(base, i)
            w = w_s[here, :]
            tan = 1.5 - w
            acc = jnp.zeros((RC, NP), F32)
            for c in range(COMP):
                rows = at(c * BW, i)
                r = r2_s[rows, :]
                acc = acc + (2.0 * r - dd[rows, pl.ds(0, NP)]) * y_s[rows, :]
            a2 = kept(5, i) / jnp.maximum(total(acc) + kept(7, i), 1.0)
            a1 = kept(4, i) + a2 * kept(6, i)
            a0 = kept(1, i) + a1 * kept(3, i)
            flow = jnp.zeros((RC, NP), F32)
            for c in range(COMP):
                rows = at(c * BW, i)
                x = a0 * r0_s[rows, :] + a1 * r1_s[rows, :] + a2 * r2_s[rows, :]
                flow = flow + prow[c, 0:RC, :] * x
                ycat[here, pl.ds(c * NP, NP)] = tan * x
            h_s[here, :] = h_s[here, :] + w * flow

        chunks(last)

        hi, lo = split2(h_s[pl.ds(pl.multiple_of(base, BW), BW), :])
        ucat[pl.ds(pl.multiple_of(base, BW), BW), :] = hi
        ucat[pl.ds(pl.multiple_of(RV + base, BW), BW), :] = lo
        first_slot = 2.0 * (NBLK - 1 - b).astype(F32)
        t8 = float(CAP) * iota((DEV, RV), 0) + first_slot
        srow = jnp.where(iota((1, RV), 1) < ((b + 1) * BW).astype(F32), slotrow[0:1, :], -1.0)
        place = jnp.concatenate(
            [jnp.where(srow == t8, 1.0, 0.0), jnp.where(srow == t8 + 1.0, 1.0, 0.0)], axis=0
        ).astype(BF)
        moved = dot(jnp.concatenate([place, place], axis=1), ucat[...])

        for k in range(NBLK):
            j = NBLK - 1 - k

            @pl.when(b == k)
            def _():
                ship[:, 2 * j, :] = moved[0:DEV]
                ship[:, 2 * j + 1, :] = moved[DEV:]
                if k == 0:
                    pl.semaphore_wait(barrier, DEV - 1)

                def send(i, c):
                    peer = lax.rem(me + i * STRIDE, DEV)
                    pltpu.make_async_remote_copy(
                        src_ref=ship.at[peer, pl.ds(2 * j, 2)],
                        dst_ref=recv.at[me, pl.ds(2 * j, 2)],
                        send_sem=send_sem.at[k],
                        recv_sem=recv_sem.at[k],
                        device_id=peer,
                        device_id_type=LOG,
                    ).start()
                    return c

                lax.fori_loop(1, DEV, send, 0, unroll=16)

        return carry

    lax.fori_loop(0, NBLK, block, 0)
    own = pltpu.make_async_copy(ship.at[me], recv.at[me], loc_sem)
    own.start()

    strain_p = dot_t(s32[...], servest[...])
    delta = jnp.zeros((8, RV), F32)
    for c in range(COMP):
        lanes = pl.ds(c * NP, NP)
        hi, lo = split2(ycat[:, lanes])
        with_hi = dot_t(gmat[:, lanes], hi)
        delta += with_hi[0:8] + with_hi[8:16] + dot_t(gmat[:, lanes], lo)[0:8]
    stress = strain_p[8:16] + strain_p[16:24] + strain_p[24:32]
    stress = stress + delta * (1.0 / math.sqrt(COMP * NODES))
    back = dot(stack(split3(stress)), servest[...])
    stress_ref[...] = (back[0:8] + back[8:16] + back[16:24])[0:VOIGT]
    own.wait()
    for k in range(NBLK):
        two_rows = pl.ds(2 * (NBLK - 1 - k), 2)
        some = pl.ds(0, DEV - 1)
        pltpu.make_async_copy(ship.at[some, two_rows], recv.at[some, two_rows], recv_sem.at[k]).wait()
        pltpu.make_async_copy(ship.at[some, two_rows], recv.at[some, two_rows], send_sem.at[k]).wait()

    def turn_out(i, carry):
        piece = recv[pl.ds(pl.multiple_of(i * 16, 16), 16)].reshape(BW, NP)
        out_ref[:, pl.ds(pl.multiple_of(i * BW, BW), BW)] = jnp.transpose(piece)[0:NODES]
        return carry

    lax.fori_loop(0, DEV // 16, turn_out, 0)


def shards(
    history, yield_flags, strain, qp_to_rve, new_owner, stiffness, pattern, coupling, plastic_dir
):
    owner = new_owner.reshape(1, RV)
    hbm = pl.BlockSpec(memory_space=pl.ANY)
    vmem = pl.BlockSpec(memory_space=pltpu.VMEM)
    v = pltpu.VMEM
    return pl.pallas_call(
        kernel,
        out_shape=(
            jax.ShapeDtypeStruct((NODES, DEV * CAP), F32),
            jax.ShapeDtypeStruct((VOIGT, RV), F32),
        ),
        in_specs=[hbm] * 6 + [pl.BlockSpec(memory_space=pltpu.SMEM)] + [hbm] * 2,
        out_specs=(vmem, vmem),
        scratch_shapes=[
            v((NODES, RV), F32), v((NODES, RV), jnp.int32), v((VOIGT, RV), F32),
            v((1, RV), jnp.int32), v((1, RV), jnp.int32), v((NB, NB, BLK, BLK), F32),
            v((COMP, VOIGT, NODES), F32), v((COMP, NODES), F32),
            v((NP, NP), F32), v((3 * NP, NP), BF), v((NP, 2 * RV), BF), v((NP, RV), BF),
            v((8, RV), F32), v((32, RV), BF), v((RV, 2 * RV), BF), v((RV, RV), BF),
            v((RV, COMP * NP), F32), v((COMP, 8, NP), F32), v((16, COMP * NP), BF),
            v((RV, NP), F32), v((RV, NP), F32),
            v((COMP * BW, NP), F32), v((COMP * BW, NP), F32), v((COMP * BW, NP), F32),
            v((COMP * BW, NP), F32), v((COMP * BW, NP), F32), v((COMP * BW, 2 * NP), F32),
            v((RV, COMP * NP), F32), v((2 * RV, NP), BF), v((8, BW, 128), F32),
            v((DEV, CAP, NP), F32), v((DEV, CAP, NP), F32),
            pltpu.SemaphoreType.DMA((8,)), pltpu.SemaphoreType.DMA(()),
            pltpu.SemaphoreType.DMA((NBLK,)), pltpu.SemaphoreType.DMA((NBLK,)),
        ],
        compiler_params=pltpu.CompilerParams(
            collective_id=0, has_side_effects=True, vmem_limit_bytes=56 * 1024 * 1024
        ),
        name="micro_newton",
    )(
        history, yield_flags, strain, qp_to_rve, owner, stiffness, pattern, coupling, plastic_dir
    )


def solution(mesh):
    both = ("macro", "pool")
    return jax.shard_map(
        shards,
        mesh=mesh,
        in_specs=(
            P(None, both), P(None, both), P(None, both), P(both, None), P(both, None),
            P(), P(), P(), P(),
        ),
        out_specs=(P(None, both), P(None, both)),
        check_vma=False,
    )
```

time: 88.7 us -> 72.5 us (0.82)
  Pallas kernels: 83.4 us -> 67.2 us
    pallas_call x1, Pallas kernels: 83.4 us -> 67.2 us  [shards(): pl.pallas_call(kernel, out_shape=(jax.ShapeDtypeStruct((NODES, DEV * CAP)...]
where the time goes in v1:
time: 72.5 us; the launch traced here: 72.3 us
  Pallas kernels  67.2 us (93%)
  local copies, waits for them, and re-layouts  4.48 us (6%)
    pallas_call x1, Pallas kernels, shards(): pl.pallas_call(kernel, out_shape=(jax.ShapeDtypeStruct((NODES, DEV * CAP)...  67.2 us
    unnamed x4, local copies, waits for them, and re-layouts  4.48 us

profile of v1, /device:TPU:1, one launch (start us, length us, event | category | flops | bytes accessed | tf_op | source)
XLA Modules:
  0.0 72.3 jit_solution(16867355303389954441)
XLA Ops:
  0.6 67.2 %micro_newton.1 = (f32[729,1024]{1,0:T(8,128)}, f32[6,512]{1,0:T(8,128)}) custom-call(f32[729,512]{1,0:T(8,128)} %hist_hbm.1, s32[729,512]{1,0:T(8,128)} %flag_hbm.1, f32[6,512]{1,0:T(8,128)} %strain_hbm.1, s32[1,512]{1,0:T(1,128)} %qp_hbm.1, s32[1,512]{1,0:T(1,128)} %bitcast.1, f32[9,9,81,81]{3,2,1,0:T(8,128)} %stiff_hbm.1, s32[9,9]{1,0:T(8,128)} %pat_ref.1, ...), custom_call_target="tpu_custom_call" | custom-call | tf_op jit(solution)/shard_map/micro_newton/pallas_call | solution.py:399
  67.8 0.0 copy-start
  67.8 3.9 %copy.13 = f32[729,1024]{1,0:T(8,128)} copy(f32[729,1024]{1,0:T(8,128)} %get-tuple-element.4) | data formatting | bytes 5971968
  71.7 0.0 copy-done
  71.7 0.6 copy.14
Async XLA Ops:
  67.8 3.9 %copy-start = (f32[6,512]{1,0:T(8,128)S(1)}, f32[6,512]{1,0:T(8,128)}, u32[]{:S(2)}) copy-start(f32[6,512]{1,0:T(8,128)} %get-tuple-element.5) | copy-start | bytes 36868

commit v2 on v1

--- a/solution.py
+++ b/solution.py
@@ -23,6 +23,7 @@
 CH = 64
 RC = 8
 UNROLL = 16
+OUTW = 256
 STRIDE = 53
 LOG = pl.DeviceIdType.LOGICAL
 F32 = jnp.float32
@@ -63,10 +64,10 @@
 
 def kernel(
     hist_hbm, flag_hbm, strain_hbm, qp_hbm, owner_hbm, stiff_hbm, pat_ref, coup_hbm, plast_hbm,
-    out_ref, stress_ref,
+    recv, stress_ref,
     hist_v, flag_v, strain_v, qp_v, owner_v, stiff_v, coup_v, plast_v,
     k32, kk, hcat, fcat, slotrow, s32, permt, servest, drive, prow, gmat,
-    h_s, w_s, r0_s, r1_s, r2_s, im0_s, y_s, dd, ycat, ucat, coef, ship, recv,
+    h_s, w_s, r0_s, r1_s, r2_s, im0_s, y_s, dd, ycat, ucat, coef, ship,
     in_sem, loc_sem, send_sem, recv_sem,
 ):
     me = lax.axis_index("macro") * 8 + lax.axis_index("pool")
@@ -381,12 +382,20 @@
         pltpu.make_async_copy(ship.at[some, two_rows], recv.at[some, two_rows], recv_sem.at[k]).wait()
         pltpu.make_async_copy(ship.at[some, two_rows], recv.at[some, two_rows], send_sem.at[k]).wait()
 
-    def turn_out(i, carry):
-        piece = recv[pl.ds(pl.multiple_of(i * 16, 16), 16)].reshape(BW, NP)
-        out_ref[:, pl.ds(pl.multiple_of(i * BW, BW), BW)] = jnp.transpose(piece)[0:NODES]
-        return carry
-
-    lax.fori_loop(0, DEV // 16, turn_out, 0)
+
+def turn(raw_ref, raw_stress_ref, out_hbm, stress_ref, buf, sem):
+    stress_ref[...] = raw_stress_ref[...]
+    copies = []
+    for i in range(DEV * CAP // OUTW):
+        for k in range(OUTW // BW):
+            first = i * OUTW + k * BW
+            piece = raw_ref[pl.ds(first // CAP, BW // CAP)].reshape(BW, NP)
+            buf[:, pl.ds(first, BW)] = jnp.transpose(piece)[0:NODES]
+        part = pl.ds(i * OUTW, OUTW)
+        copies.append(pltpu.make_async_copy(buf.at[:, part], out_hbm.at[:, part], sem.at[i]))
+        copies[i].start()
+    for copy in copies:
+        copy.wait()
 
 
 def shards(
@@ -396,11 +405,11 @@
     hbm = pl.BlockSpec(memory_space=pl.ANY)
     vmem = pl.BlockSpec(memory_space=pltpu.VMEM)
     v = pltpu.VMEM
-    return pl.pallas_call(
+    raw, raw_stress = pl.pallas_call(
         kernel,
         out_shape=(
-            jax.ShapeDtypeStruct((NODES, DEV * CAP), F32),
-            jax.ShapeDtypeStruct((VOIGT, RV), F32),
+            v((DEV, CAP, NP), F32),
+            v((VOIGT, RV), F32),
         ),
         in_specs=[hbm] * 6 + [pl.BlockSpec(memory_space=pltpu.SMEM)] + [hbm] * 2,
         out_specs=(vmem, vmem),
@@ -415,7 +424,7 @@
             v((COMP * BW, NP), F32), v((COMP * BW, NP), F32), v((COMP * BW, NP), F32),
             v((COMP * BW, NP), F32), v((COMP * BW, NP), F32), v((COMP * BW, 2 * NP), F32),
             v((RV, COMP * NP), F32), v((2 * RV, NP), BF), v((8, BW, 128), F32),
-            v((DEV, CAP, NP), F32), v((DEV, CAP, NP), F32),
+            v((DEV, CAP, NP), F32),
             pltpu.SemaphoreType.DMA((8,)), pltpu.SemaphoreType.DMA(()),
             pltpu.SemaphoreType.DMA((NBLK,)), pltpu.SemaphoreType.DMA((NBLK,)),
         ],
@@ -426,6 +435,20 @@
     )(
         history, yield_flags, strain, qp_to_rve, owner, stiffness, pattern, coupling, plastic_dir
     )
+    return pl.pallas_call(
+        turn,
+        out_shape=(
+            jax.ShapeDtypeStruct((NODES, DEV * CAP), F32),
+            jax.ShapeDtypeStruct((VOIGT, RV), F32),
+        ),
+        in_specs=[vmem, vmem],
+        out_specs=(hbm, vmem),
+        scratch_shapes=[
+            v((NODES, DEV * CAP), F32), pltpu.SemaphoreType.DMA((DEV * CAP // OUTW,)),
+        ],
+        compiler_params=pltpu.CompilerParams(vmem_limit_bytes=16 * 1024 * 1024),
+        name="turn_history",
+    )(raw, raw_stress)
 
 
 def solution(mesh):

time: 72.5 us -> 67.5 us (0.931)
  local copies, waits for them, and re-layouts: 4.48 us -> 0 us
    unnamed x4 -> x0, local copies, waits for them, and re-layouts: 4.48 us -> none
    pallas_call x1 -> x2, Pallas kernels: 67.2 us -> 66.7 us  [the longest x1 64.2 us: shards(): pl.pallas_call(kernel, out_shape=(v((DEV, CAP, NP), F32), v((VOIGT, RV),...]
where the time goes in v2:
time: 67.5 us; the launch traced here: 67.4 us
  Pallas kernels  66.7 us (99%)
    pallas_call x1, Pallas kernels, shards(): pl.pallas_call(kernel, out_shape=(v((DEV, CAP, NP), F32), v((VOIGT, RV),...  64.2 us
    pallas_call x1, Pallas kernels, shards(): pl.pallas_call(turn, out_shape=(jax.ShapeDtypeStruct((NODES, DEV * CAP),...  2.52 us

profile of v2, /device:TPU:1, one launch (start us, length us, event | category | flops | bytes accessed | tf_op | source)
XLA Modules:
  0.0 67.4 jit_solution(2657853060010933875)
XLA Ops:
  0.6 64.2 %micro_newton.1 = (f32[128,8,768]{2,1,0:T(8,128)S(1)}, f32[6,512]{1,0:T(8,128)S(1)}) custom-call(f32[729,512]{1,0:T(8,128)} %hist_hbm.1, s32[729,512]{1,0:T(8,128)} %flag_hbm.1, f32[6,512]{1,0:T(8,128)} %strain_hbm.1, s32[1,512]{1,0:T(1,128)} %qp_hbm.1, s32[1,512]{1,0:T(1,128)} %bitcast.1, f32[9,9,81,81]{3,2,1,0:T(8,128)} %stiff_hbm.1, s32[9,9]{1,0:T(8,128)} %pat_ref.1, ...), custom_call_target="tpu_custom_call" | custom-call | tf_op jit(solution)/shard_map/micro_newton/pallas_call | solution.py:408
  64.9 2.5 %turn_history.1 = (f32[729,1024]{1,0:T(8,128)}, f32[6,512]{1,0:T(8,128)}) custom-call(f32[128,8,768]{2,1,0:T(8,128)S(1)} %get-tuple-element.4.raw_ref, f32[6,512]{1,0:T(8,128)S(1)} %get-tuple-element.5.raw_stress_ref), custom_call_target="tpu_custom_call" | custom-call | tf_op jit(solution)/shard_map/turn_history/pallas_call | solution.py:438

commit v3 on v2

--- a/solution.py
+++ b/solution.py
@@ -67,7 +67,7 @@
     recv, stress_ref,
     hist_v, flag_v, strain_v, qp_v, owner_v, stiff_v, coup_v, plast_v,
     k32, kk, hcat, fcat, slotrow, s32, permt, servest, drive, prow, gmat,
-    h_s, w_s, r0_s, r1_s, r2_s, im0_s, y_s, dd, ycat, ucat, coef, ship,
+    h_s, w_s, r0_s, r1_s, r2_s, im0_s, y_s, ycat, ucat, coef, sums, ship,
     in_sem, loc_sem, send_sem, recv_sem,
 ):
     me = lax.axis_index("macro") * 8 + lax.axis_index("pool")
@@ -181,7 +181,6 @@
         return carry
 
     lax.fori_loop(0, NP // CH, split_k, 0)
-    ucat[...] = jnp.zeros_like(ucat)
 
     def chunks(body):
         def step(i, carry):
@@ -193,23 +192,17 @@
     def at(base, i):
         return pl.ds(pl.multiple_of(base + i * RC, RC), RC)
 
-    def total(acc):
+    def partial(k, i, acc):
         part = acc[:, 0:128]
-        for k in range(1, NP // 128):
-            part = part + acc[:, k * 128 : (k + 1) * 128]
-        return jnp.sum(part, axis=1, keepdims=True)
-
-    def keep(k, i, col):
-        coef[k, at(0, i), :] = jnp.broadcast_to(col, (RC, 128))
-
-    def kept(k, i):
-        return coef[k, at(0, i), 0:1]
-
-    def put(rows, v, low=True):
-        hi = v.astype(BF).astype(F32)
-        dd[rows, pl.ds(0, NP)] = hi
-        if low:
-            dd[rows, pl.ds(NP, NP)] = v - hi
+        for n in range(1, NP // 128):
+            part = part + acc[:, n * 128 : (n + 1) * 128]
+        sums[k, at(0, i), :] = part
+
+    def total(k):
+        return jnp.broadcast_to(jnp.sum(sums[k], axis=1, keepdims=True), (BW, 128))
+
+    def wide(k, i):
+        return jnp.concatenate([coef[k, at(0, i), :]] * (NP // 128), axis=1)
 
     def block(b, carry):
         base = b * BW
@@ -226,97 +219,115 @@
                 rows = at(c * BW, i)
                 v = drive[here, pl.ds(c * NP, NP)] - wh * prow[c, 0:RC, :]
                 r0_s[rows, :] = v
-                put(rows, v)
                 acc = acc + v * v
-            keep(0, i, total(acc))
+            partial(0, i, acc)
 
         chunks(source)
 
-        def product(parts):
-            left = dd[...].astype(BF)
-            hi = left[:, 0:NP]
-            cat = [hi, hi] + ([left[:, NP:]] if parts == 3 else [])
+        def product(ref, parts):
+            v = ref[...]
+            hi = v.astype(BF)
+            cat = [hi, hi]
+            if parts == 3:
+                cat.append((v - hi.astype(F32)).astype(BF))
             return dot(jnp.concatenate(cat, axis=1), kk[0 : parts * NP, :])
 
-        im0_s[...] = product(3)
+        im0_s[...] = product(r0_s, 3)
 
         def first(i):
             tan = 1.5 - w_s[at(base, i), :]
             acc = jnp.zeros((RC, NP), F32)
-            ims = []
             for c in range(COMP):
                 rows = at(c * BW, i)
                 r = r0_s[rows, :]
                 im = im0_s[rows, :] + tan * r
                 im0_s[rows, :] = im
-                ims.append(im)
                 acc = acc + r * im
-            rr = kept(0, i)
-            size = rr / jnp.maximum(total(acc), 1.0)
+            partial(1, i, acc)
+
+        chunks(first)
+        norm0 = total(0)
+        size0 = norm0 / jnp.maximum(total(1), 1.0)
+        coef[0] = size0
+
+        def first_step(i):
+            size = wide(0, i)
             acc = jnp.zeros((RC, NP), F32)
             for c in range(COMP):
                 rows = at(c * BW, i)
-                r = r0_s[rows, :] - size * ims[c]
+                r = r0_s[rows, :] - size * im0_s[rows, :]
                 r1_s[rows, :] = r
-                put(rows, r)
                 acc = acc + r * r
-            after = total(acc)
-            keep(1, i, size)
-            keep(2, i, after)
-            keep(3, i, after / jnp.maximum(rr, 1.0))
-
-        chunks(first)
-        y_s[...] = product(3)
+            partial(2, i, acc)
+
+        chunks(first_step)
+        y_s[...] = product(r1_s, 3)
+        norm1 = total(2)
+        ratio0 = norm1 / jnp.maximum(norm0, 1.0)
+        coef[1] = ratio0
 
         def second(i):
             tan = 1.5 - w_s[at(base, i), :]
-            ratio = kept(3, i)
+            ratio = wide(1, i)
             acc = jnp.zeros((RC, NP), F32)
-            ims = []
             for c in range(COMP):
                 rows = at(c * BW, i)
                 r = r1_s[rows, :]
                 im = y_s[rows, :] + tan * r + ratio * im0_s[rows, :]
-                ims.append(im)
+                y_s[rows, :] = im
                 acc = acc + (r + ratio * r0_s[rows, :]) * im
-            rr = kept(2, i)
-            energy = total(acc)
-            size = rr / jnp.maximum(energy, 1.0)
+            partial(3, i, acc)
+
+        chunks(second)
+        energy = total(3)
+        size1 = norm1 / jnp.maximum(energy, 1.0)
+        coef[2] = size1
+
+        def second_step(i):
+            size = wide(2, i)
             sq = jnp.zeros((RC, NP), F32)
             cross = jnp.zeros((RC, NP), F32)
             for c in range(COMP):
                 rows = at(c * BW, i)
-                r = r1_s[rows, :] - size * ims[c]
+                im = y_s[rows, :]
+                r = r1_s[rows, :] - size * im
                 r2_s[rows, :] = r
-                put(rows, r, low=False)
                 sq = sq + r * r
-                cross = cross + r * ims[c]
-            after = total(sq)
-            ratio = after / jnp.maximum(rr, 1.0)
-            keep(4, i, size)
-            keep(5, i, after)
-            keep(6, i, ratio)
-            keep(7, i, total(tan * sq) + ratio * (2.0 * total(cross) + ratio * energy))
-
-        chunks(second)
-        y_s[...] = product(2)
+                cross = cross + r * im
+            partial(4, i, sq)
+            partial(5, i, cross)
+            partial(6, i, (1.5 - w_s[at(base, i), :]) * sq)
+
+        chunks(second_step)
+        y_s[...] = product(r2_s, 2)
+        norm2 = total(4)
+        ratio1 = norm2 / jnp.maximum(norm1, 1.0)
+        rest = total(6) + ratio1 * (2.0 * total(5) + ratio1 * energy)
+
+        def third(i):
+            acc = jnp.zeros((RC, NP), F32)
+            for c in range(COMP):
+                rows = at(c * BW, i)
+                r = r2_s[rows, :]
+                acc = acc + (2.0 * r - r.astype(BF).astype(F32)) * y_s[rows, :]
+            partial(7, i, acc)
+
+        chunks(third)
+        a2 = norm2 / jnp.maximum(total(7) + rest, 1.0)
+        a1 = size1 + a2 * ratio1
+        coef[3] = size0 + a1 * ratio0
+        coef[4] = a1
+        coef[5] = a2
 
         def last(i):
             here = at(base, i)
             w = w_s[here, :]
             tan = 1.5 - w
-            acc = jnp.zeros((RC, NP), F32)
-            for c in range(COMP):
-                rows = at(c * BW, i)
-                r = r2_s[rows, :]
-                acc = acc + (2.0 * r - dd[rows, pl.ds(0, NP)]) * y_s[rows, :]
-            a2 = kept(5, i) / jnp.maximum(total(acc) + kept(7, i), 1.0)
-            a1 = kept(4, i) + a2 * kept(6, i)
-            a0 = kept(1, i) + a1 * kept(3, i)
+            a = [wide(3 + k, i) for k in range(3)]
             flow = jnp.zeros((RC, NP), F32)
             for c in range(COMP):
                 rows = at(c * BW, i)
-                x = a0 * r0_s[rows, :] + a1 * r1_s[rows, :] + a2 * r2_s[rows, :]
+                x = a[0] * r0_s[rows, :] + a[1] * r1_s[rows, :] + a[2] * r2_s[rows, :]
                 flow = flow + prow[c, 0:RC, :] * x
                 ycat[here, pl.ds(c * NP, NP)] = tan * x
             h_s[here, :] = h_s[here, :] + w * flow
@@ -324,21 +335,24 @@
         chunks(last)
 
         hi, lo = split2(h_s[pl.ds(pl.multiple_of(base, BW), BW), :])
-        ucat[pl.ds(pl.multiple_of(base, BW), BW), :] = hi
-        ucat[pl.ds(pl.multiple_of(RV + base, BW), BW), :] = lo
-        first_slot = 2.0 * (NBLK - 1 - b).astype(F32)
-        t8 = float(CAP) * iota((DEV, RV), 0) + first_slot
-        srow = jnp.where(iota((1, RV), 1) < ((b + 1) * BW).astype(F32), slotrow[0:1, :], -1.0)
-        place = jnp.concatenate(
-            [jnp.where(srow == t8, 1.0, 0.0), jnp.where(srow == t8 + 1.0, 1.0, 0.0)], axis=0
-        ).astype(BF)
-        moved = dot(jnp.concatenate([place, place], axis=1), ucat[...])
+        ucat[pl.ds(pl.multiple_of(2 * base, BW), BW), :] = hi
+        ucat[pl.ds(pl.multiple_of(2 * base + BW, BW), BW), :] = lo
 
         for k in range(NBLK):
             j = NBLK - 1 - k
 
             @pl.when(b == k)
             def _():
+                t8 = float(CAP) * iota((DEV, BW), 0) + 2.0 * j
+                parts = []
+                for n in range(k + 1):
+                    srow = slotrow[0:1, n * BW : (n + 1) * BW]
+                    one = jnp.concatenate(
+                        [jnp.where(srow == t8, 1.0, 0.0), jnp.where(srow == t8 + 1.0, 1.0, 0.0)],
+                        axis=0,
+                    ).astype(BF)
+                    parts += [one, one]
+                moved = dot(jnp.concatenate(parts, axis=1), ucat[0 : 2 * (k + 1) * BW, :])
                 ship[:, 2 * j, :] = moved[0:DEV]
                 ship[:, 2 * j + 1, :] = moved[DEV:]
                 if k == 0:
@@ -356,7 +370,7 @@
                     ).start()
                     return c
 
-                lax.fori_loop(1, DEV, send, 0, unroll=16)
+                lax.fori_loop(1, DEV, send, 0, unroll=127)
 
         return carry
 
@@ -422,8 +436,8 @@
             v((RV, COMP * NP), F32), v((COMP, 8, NP), F32), v((16, COMP * NP), BF),
             v((RV, NP), F32), v((RV, NP), F32),
             v((COMP * BW, NP), F32), v((COMP * BW, NP), F32), v((COMP * BW, NP), F32),
-            v((COMP * BW, NP), F32), v((COMP * BW, NP), F32), v((COMP * BW, 2 * NP), F32),
-            v((RV, COMP * NP), F32), v((2 * RV, NP), BF), v((8, BW, 128), F32),
+            v((COMP * BW, NP), F32), v((COMP * BW, NP), F32),
+            v((RV, COMP * NP), F32), v((2 * RV, NP), BF), v((6, BW, 128), F32), v((8, BW, 128), F32),
             v((DEV, CAP, NP), F32),
             pltpu.SemaphoreType.DMA((8,)), pltpu.SemaphoreType.DMA(()),
             pltpu.SemaphoreType.DMA((NBLK,)), pltpu.SemaphoreType.DMA((NBLK,)),

time: 67.5 us -> 63.2 us (0.936)
  Pallas kernels: 66.7 us -> 62.3 us
    pallas_call x1, Pallas kernels: 64.2 us -> 59.8 us  [shards(): pl.pallas_call(kernel, out_shape=(v((DEV, CAP, NP), F32), v((VOIGT, RV),...]
where the time goes in v3:
time: 63.2 us; the launch traced here: 63.1 us
  Pallas kernels  62.3 us (99%)
  between operations  0.8 us (1%)
    pallas_call x1, Pallas kernels, shards(): pl.pallas_call(kernel, out_shape=(v((DEV, CAP, NP), F32), v((VOIGT, RV),...  59.8 us
    pallas_call x1, Pallas kernels, shards(): pl.pallas_call(turn, out_shape=(jax.ShapeDtypeStruct((NODES, DEV * CAP),...  2.52 us

profile of v3, /device:TPU:1, one launch (start us, length us, event | category | flops | bytes accessed | tf_op | source)
XLA Modules:
  0.0 63.1 jit_solution(7273667955913372021)
XLA Ops:
  0.6 59.8 %micro_newton.1 = (f32[128,8,768]{2,1,0:T(8,128)S(1)}, f32[6,512]{1,0:T(8,128)S(1)}) custom-call(f32[729,512]{1,0:T(8,128)} %hist_hbm.1, s32[729,512]{1,0:T(8,128)} %flag_hbm.1, f32[6,512]{1,0:T(8,128)} %strain_hbm.1, s32[1,512]{1,0:T(1,128)} %qp_hbm.1, s32[1,512]{1,0:T(1,128)} %bitcast.1, f32[9,9,81,81]{3,2,1,0:T(8,128)} %stiff_hbm.1, s32[9,9]{1,0:T(8,128)} %pat_ref.1, ...), custom_call_target="tpu_custom_call" | custom-call | tf_op jit(solution)/shard_map/micro_newton/pallas_call | solution.py:422
  60.4 2.5 %turn_history.1 = (f32[729,1024]{1,0:T(8,128)}, f32[6,512]{1,0:T(8,128)}) custom-call(f32[128,8,768]{2,1,0:T(8,128)S(1)} %get-tuple-element.4.raw_ref, f32[6,512]{1,0:T(8,128)S(1)} %get-tuple-element.5.raw_stress_ref), custom_call_target="tpu_custom_call" | custom-call | tf_op jit(solution)/shard_map/turn_history/pallas_call | solution.py:452

commit v4 on v3

--- a/solution.py
+++ b/solution.py
@@ -18,13 +18,15 @@
 RV = 512
 BW = 128
 NBLK = RV // BW
-DEV = 128
+MACRO = 16
+POOL = 8
+DEV = MACRO * POOL
 CAP = 8
 CH = 64
 RC = 8
 UNROLL = 16
 OUTW = 256
-STRIDE = 53
+STRIDE = 77
 LOG = pl.DeviceIdType.LOGICAL
 F32 = jnp.float32
 BF = jnp.bfloat16
@@ -68,27 +70,47 @@
     hist_v, flag_v, strain_v, qp_v, owner_v, stiff_v, coup_v, plast_v,
     k32, kk, hcat, fcat, slotrow, s32, permt, servest, drive, prow, gmat,
     h_s, w_s, r0_s, r1_s, r2_s, im0_s, y_s, ycat, ucat, coef, sums, ship,
-    in_sem, loc_sem, send_sem, recv_sem,
+    in_sem, loc_sem, send_sem, recv_sem, column_sem,
 ):
-    me = lax.axis_index("macro") * 8 + lax.axis_index("pool")
-    pairs = (
-        (owner_hbm, owner_v), (qp_hbm, qp_v), (stiff_hbm, stiff_v), (hist_hbm, hist_v),
-        (flag_hbm, flag_v), (strain_hbm, strain_v), (coup_hbm, coup_v), (plast_hbm, plast_v),
-    )
-    loads = [pltpu.make_async_copy(a, b, in_sem.at[i]) for i, (a, b) in enumerate(pairs)]
-    for load in loads:
-        load.start()
+    me = lax.axis_index("macro") * POOL + lax.axis_index("pool")
+    loads = {}
+
+    def load(name, src, dst, sem):
+        loads.setdefault(name, []).append(pltpu.make_async_copy(src, dst, in_sem.at[sem]))
+        loads[name][-1].start()
+
+    def loaded(*names):
+        for name in names:
+            for copy in loads[name]:
+                copy.wait()
+
+    load("owner", owner_hbm, owner_v, 0)
+    load("qp", qp_hbm, qp_v, 1)
+    load("small", strain_hbm, strain_v, 2)
+    load("small", coup_hbm, coup_v, 3)
+    load("small", plast_hbm, plast_v, 4)
+    for i, (start, size) in enumerate(((0, 256), (256, 256), (512, NODES - 512))):
+        rows = pl.ds(start, size)
+        load("hist", hist_hbm.at[rows], hist_v.at[rows], 5 + i)
+        load("flag", flag_hbm.at[rows], flag_v.at[rows], 8 + i)
+    for a in range(NB):
+        load("stiff%d" % a, stiff_hbm.at[a], stiff_v.at[a], 11 + a)
 
     barrier = pltpu.get_barrier_semaphore()
 
-    def greet(i, carry):
-        pl.semaphore_signal(barrier, inc=1, device_id=lax.rem(me + i, DEV), device_id_type=LOG)
-        return carry
-
-    lax.fori_loop(1, DEV, greet, 0)
-
-    loads[0].wait()
-    loads[1].wait()
+    macro, pool = lax.axis_index("macro"), lax.axis_index("pool")
+
+    def greet(sem, other_macro, other_pool):
+        pl.semaphore_signal(
+            sem, inc=1, device_id=other_macro * POOL + other_pool, device_id_type=LOG
+        )
+
+    for i in range(1, POOL):
+        greet(barrier, macro, lax.rem(pool + i, POOL))
+    for i in range(1, MACRO):
+        greet(barrier, lax.rem(macro + i, MACRO), pool)
+
+    loaded("owner", "qp")
     owner_row = owner_v[...].astype(F32)
     owner_col = to_columns(owner_row)
     qp_row = qp_v[...].astype(F32)
@@ -126,8 +148,7 @@
         hit = e_of == qp_row[:, t * BW : (t + 1) * BW]
         servest[:, lanes] = jnp.where(hit, 1.0, 0.0).astype(BF)
 
-    for i in range(5, 8):
-        loads[i].wait()
+    loaded("small")
     shi, smid, slo = split3(jnp.concatenate([strain_v[...], jnp.zeros((2, RV), F32)], axis=0))
     s32[...] = stack([shi, shi, smid, slo])
     strain_t = dot_t(servest[...], s32[...]).astype(BF)
@@ -144,8 +165,7 @@
         prow[c] = jnp.broadcast_to(line, (8, NP))
     drive[...] = dot(strain_t, jnp.concatenate(cols, axis=1).astype(BF))
 
-    loads[3].wait()
-    loads[4].wait()
+    loaded("hist", "flag")
     hcat[pl.ds(NP - 64, 64), :] = jnp.zeros((64, 2 * RV), BF)
     fcat[pl.ds(NP - 64, 64), :] = jnp.zeros((64, RV), BF)
 
@@ -167,9 +187,13 @@
     h_s[...] = dot_t(permt[...], hcat[...])
     w_s[...] = dot_t(permt[:, 0:RV], fcat[...])
 
+    pl.semaphore_wait(barrier, POOL + MACRO - 2)
+    for i in range(1, MACRO):
+        greet(column_sem, lax.rem(macro + i, MACRO), pool)
+
     k32[...] = jnp.zeros_like(k32)
-    loads[2].wait()
     for a in range(NB):
+        loaded("stiff%d" % a)
         row = [stiff_v[a, b] * pat_ref[a, b].astype(F32) for b in range(NB)]
         k32[pl.ds(a * BLK, BLK), pl.ds(0, NODES)] = jnp.concatenate(row, axis=1)
 
@@ -356,7 +380,7 @@
                 ship[:, 2 * j, :] = moved[0:DEV]
                 ship[:, 2 * j + 1, :] = moved[DEV:]
                 if k == 0:
-                    pl.semaphore_wait(barrier, DEV - 1)
+                    pl.semaphore_wait(column_sem, MACRO - 1)
 
                 def send(i, c):
                     peer = lax.rem(me + i * STRIDE, DEV)
@@ -439,8 +463,9 @@
             v((COMP * BW, NP), F32), v((COMP * BW, NP), F32),
             v((RV, COMP * NP), F32), v((2 * RV, NP), BF), v((6, BW, 128), F32), v((8, BW, 128), F32),
             v((DEV, CAP, NP), F32),
-            pltpu.SemaphoreType.DMA((8,)), pltpu.SemaphoreType.DMA(()),
+            pltpu.SemaphoreType.DMA((20,)), pltpu.SemaphoreType.DMA(()),
             pltpu.SemaphoreType.DMA((NBLK,)), pltpu.SemaphoreType.DMA((NBLK,)),
+            pltpu.SemaphoreType.REGULAR,
         ],
         compiler_params=pltpu.CompilerParams(
             collective_id=0, has_side_effects=True, vmem_limit_bytes=56 * 1024 * 1024

time: 63.2 us -> 61.2 us (0.968)
  Pallas kernels: 62.3 us -> 60.2 us
    pallas_call x1, Pallas kernels: 59.8 us -> 57.7 us  [shards(): pl.pallas_call(kernel, out_shape=(v((DEV, CAP, NP), F32), v((VOIGT, RV),...]
where the time goes in v4:
time: 61.2 us; the launch traced here: 61 us
  Pallas kernels  60.2 us (98%)
  between operations  0.8 us (1%)
    pallas_call x1, Pallas kernels, shards(): pl.pallas_call(kernel, out_shape=(v((DEV, CAP, NP), F32), v((VOIGT, RV),...  57.7 us
    pallas_call x1, Pallas kernels, shards(): pl.pallas_call(turn, out_shape=(jax.ShapeDtypeStruct((NODES, DEV * CAP),...  2.52 us

profile of v4, /device:TPU:1, one launch (start us, length us, event | category | flops | bytes accessed | tf_op | source)
XLA Modules:
  0.0 61.0 jit_solution(9487484928985900965)
XLA Ops:
  0.6 57.7 %micro_newton.1 = (f32[128,8,768]{2,1,0:T(8,128)S(1)}, f32[6,512]{1,0:T(8,128)S(1)}) custom-call(f32[729,512]{1,0:T(8,128)} %hist_hbm.1, s32[729,512]{1,0:T(8,128)} %flag_hbm.1, f32[6,512]{1,0:T(8,128)} %strain_hbm.1, s32[1,512]{1,0:T(1,128)} %qp_hbm.1, s32[1,512]{1,0:T(1,128)} %bitcast.1, f32[9,9,81,81]{3,2,1,0:T(8,128)} %stiff_hbm.1, s32[9,9]{1,0:T(8,128)} %pat_ref.1, ...), custom_call_target="tpu_custom_call" | custom-call | tf_op jit(solution)/shard_map/micro_newton/pallas_call | solution.py:446
  58.3 2.5 %turn_history.1 = (f32[729,1024]{1,0:T(8,128)}, f32[6,512]{1,0:T(8,128)}) custom-call(f32[128,8,768]{2,1,0:T(8,128)S(1)} %get-tuple-element.4.raw_ref, f32[6,512]{1,0:T(8,128)S(1)} %get-tuple-element.5.raw_stress_ref), custom_call_target="tpu_custom_call" | custom-call | tf_op jit(solution)/shard_map/turn_history/pallas_call | solution.py:477

commit v5 on v4

--- a/solution.py
+++ b/solution.py
@@ -26,7 +26,7 @@
 RC = 8
 UNROLL = 16
 OUTW = 256
-STRIDE = 77
+STRIDE = 109
 LOG = pl.DeviceIdType.LOGICAL
 F32 = jnp.float32
 BF = jnp.bfloat16

time: 61.2 us -> 62.5 us (1.021)
  Pallas kernels: 60.2 us -> 61.5 us
    pallas_call x1, Pallas kernels: 57.7 us -> 59 us  [shards(): pl.pallas_call(kernel, out_shape=(v((DEV, CAP, NP), F32), v((VOIGT, RV),...]
where the time goes in v5:
time: 62.5 us; the launch traced here: 62.3 us
  Pallas kernels  61.5 us (98%)
  between operations  0.8 us (1%)
    pallas_call x1, Pallas kernels, shards(): pl.pallas_call(kernel, out_shape=(v((DEV, CAP, NP), F32), v((VOIGT, RV),...  59 us
    pallas_call x1, Pallas kernels, shards(): pl.pallas_call(turn, out_shape=(jax.ShapeDtypeStruct((NODES, DEV * CAP),...  2.52 us

profile of v5, /device:TPU:1, one launch (start us, length us, event | category | flops | bytes accessed | tf_op | source)
XLA Modules:
  0.0 62.3 jit_solution(1241910805536819659)
XLA Ops:
  0.6 59.0 %micro_newton.1 = (f32[128,8,768]{2,1,0:T(8,128)S(1)}, f32[6,512]{1,0:T(8,128)S(1)}) custom-call(f32[729,512]{1,0:T(8,128)} %hist_hbm.1, s32[729,512]{1,0:T(8,128)} %flag_hbm.1, f32[6,512]{1,0:T(8,128)} %strain_hbm.1, s32[1,512]{1,0:T(1,128)} %qp_hbm.1, s32[1,512]{1,0:T(1,128)} %bitcast.1, f32[9,9,81,81]{3,2,1,0:T(8,128)} %stiff_hbm.1, s32[9,9]{1,0:T(8,128)} %pat_ref.1, ...), custom_call_target="tpu_custom_call" | custom-call | tf_op jit(solution)/shard_map/micro_newton/pallas_call | solution.py:446
  59.6 2.5 %turn_history.1 = (f32[729,1024]{1,0:T(8,128)}, f32[6,512]{1,0:T(8,128)}) custom-call(f32[128,8,768]{2,1,0:T(8,128)S(1)} %get-tuple-element.4.raw_ref, f32[6,512]{1,0:T(8,128)S(1)} %get-tuple-element.5.raw_stress_ref), custom_call_target="tpu_custom_call" | custom-call | tf_op jit(solution)/shard_map/turn_history/pallas_call | solution.py:477
